TPU v7x, 768 devices: a whole 4x8x12 slice. The times are simulated.
768 devices in a mesh: pipe: 12 (over z), ep: 64 (over y, x, core).
Axes of the slice: x: 4, y: 8, z: 12, core: 2. Of those that a mesh axis runs over, the one named last changes fastest.
Arguments:
- activations: bfloat16 [12, 192, 7168], P('pipe', 'ep'), may hold values from -6 to 6
- cotangent: bfloat16 [12, 192, 7168], P('pipe', 'ep'), may hold values from -6 to 6
- forward_experts: int32 [12, 192, 4], P('pipe', 'ep'), may hold values from 0 to 7, all different within a row; in each aligned block of 3 rows (0 to 2, 3 to 5, ..., all dimensions but the last counted through in order) at most 2 rows name the same one
- forward_weights: float32 [12, 192, 4], P('pipe', 'ep'), may hold values from 0.2 to 1
- backward_experts: int32 [12, 192, 4], P('pipe', 'ep'), may hold values from 0 to 7, all different within a row; in each aligned block of 3 rows (0 to 2, 3 to 5, ..., all dimensions but the last counted through in order) at most 2 rows name the same one
- backward_weights: float32 [12, 192, 4], P('pipe', 'ep'), may hold values from 0.2 to 1
- gate_weight: bfloat16 [7168, 16384], P(None, 'ep'), may hold values from -0.0625 to 0.0625
- up_weight: bfloat16 [7168, 16384], P(None, 'ep'), may hold values from -0.0625 to 0.0625
- down_weight: bfloat16 [16384, 7168], P('ep'), may hold values from -0.125 to 0.125
- saved_gate: bfloat16 [12, 128, 16384], P('pipe', None, 'ep'), may hold values from -6 to 6
- saved_up: bfloat16 [12, 128, 16384], P('pipe', None, 'ep'), may hold values from -6 to 6
Outputs:
- input_handoff: bfloat16 [12, 192, 7168], P('pipe', 'ep')
- grad_handoff: bfloat16 [12, 192, 7168], P('pipe', 'ep')
Inputs may be any that keep to these rules, and one draw needn't show every extreme that they name: `forward_experts`: each token names 4 different experts. Within the 3 tokens of one device at one section, no expert is named more than 2 times, and some device names some expert exactly 2 times. `backward_experts`: each token names 4 different experts. Within the 3 tokens of one device at one section, no expert is named more than 2 times, and some device names some expert exactly 2 times.
All inputs are finite; a program needn't handle non-finite values.
Results may differ from a plain program's by a relative error of at most 0.0058.
Values may be sent and summed in bfloat16 or wider, within the bound.
A program may use at most 128 MiB of HBM per device.

v0:
```python
import jax
import jax.numpy as jnp
from jax import lax
from jax.sharding import PartitionSpec as P

EXPERTS = 8
TOP = 4
CAP = 2


def from_behind(shard, axis, by):
    devices = lax.axis_size(axis)
    pairs = [(i, i + by) for i in range(devices) if 0 <= i + by < devices]
    return lax.ppermute(shard, axis, pairs)


def slot_table(expert_ids):
    flat_ids = expert_ids.reshape(-1)
    onehot = (flat_ids[:, None] == jnp.arange(EXPERTS, dtype=jnp.int32)[None, :]).astype(jnp.int32)
    before = jnp.cumsum(onehot, axis=0) - onehot
    position = jnp.sum(before * onehot, axis=1)
    return flat_ids * CAP + position


def pack_slots(slot_values, target):
    places = jnp.arange(EXPERTS * CAP, dtype=jnp.int32)
    select = (places[:, None] == target[None, :]).astype(jnp.bfloat16)
    return jnp.dot(select, slot_values, preferred_element_type=jnp.float32).astype(jnp.bfloat16)


def route_slots(compact, expert_work, shards):
    model_width = compact.shape[1]
    spread_rows = jnp.broadcast_to(
        compact.reshape(EXPERTS, 1, CAP, model_width), (EXPERTS, shards, CAP, model_width)
    ).reshape(EXPERTS * shards * CAP, model_width)
    arrived = lax.all_to_all(spread_rows, "ep", split_axis=0, concat_axis=0, tiled=True)
    results = expert_work(arrived, 0)
    returned = lax.all_to_all(results, "ep", split_axis=0, concat_axis=0, tiled=True)
    summed = jnp.sum(
        returned.astype(jnp.float32).reshape(EXPERTS, shards, CAP, model_width), axis=1
    )
    return summed.reshape(EXPERTS * CAP, model_width)


def body(
    activations,
    cotangent,
    forward_experts,
    forward_weights,
    backward_experts,
    backward_weights,
    gate_weight,
    up_weight,
    down_weight,
    saved_gate,
    saved_up,
):
    shards = lax.axis_size("ep") // EXPERTS
    model_width = activations.shape[2]
    contract_last = (((1,), (1,)), ((), ()))

    def expert_forward(slot_rows, first_row):
        gate_pre = jnp.dot(slot_rows, gate_weight, preferred_element_type=jnp.float32)
        up_pre = jnp.dot(slot_rows, up_weight, preferred_element_type=jnp.float32)
        hidden = (jax.nn.silu(gate_pre) * up_pre).astype(jnp.bfloat16)
        return jnp.dot(hidden, down_weight, preferred_element_type=jnp.float32).astype(jnp.bfloat16)

    def expert_backward(slot_rows, first_row):
        row_count = slot_rows.shape[0]
        gate_value = saved_gate[0].astype(jnp.float32)
        up_value = saved_up[0].astype(jnp.float32)
        grad_hidden = lax.dot_general(
            slot_rows, down_weight, contract_last, preferred_element_type=jnp.float32
        )
        sigmoid_gate = jax.nn.sigmoid(gate_value)
        gate_grad = (
            grad_hidden * up_value * sigmoid_gate * (1.0 + gate_value * (1.0 - sigmoid_gate))
        ).astype(jnp.bfloat16)
        up_grad = (grad_hidden * (gate_value * sigmoid_gate)).astype(jnp.bfloat16)
        back_rows = lax.dot_general(
            gate_grad, gate_weight, contract_last, preferred_element_type=jnp.float32
        )
        back_rows = back_rows + lax.dot_general(
            up_grad, up_weight, contract_last, preferred_element_type=jnp.float32
        )
        return back_rows.astype(jnp.bfloat16)

    token_rows = activations[0]
    target_ahead = slot_table(forward_experts[0])
    compact_ahead = pack_slots(jnp.repeat(token_rows, TOP, axis=0), target_ahead)
    combined_ahead = route_slots(compact_ahead, expert_forward, shards)
    picked_ahead = jnp.take(combined_ahead, target_ahead, axis=0) * forward_weights[0].reshape(
        -1, 1
    )
    layer_out = token_rows.astype(jnp.float32) + jnp.sum(
        picked_ahead.reshape(-1, TOP, model_width), axis=1
    )
    input_handoff = from_behind(layer_out.astype(jnp.bfloat16)[None], "pipe", 1)
    grad_rows = cotangent[0].astype(jnp.float32)
    target_behind = slot_table(backward_experts[0])
    scaled = (backward_weights[0].reshape(-1, 1) * jnp.repeat(grad_rows, TOP, axis=0)).astype(
        jnp.bfloat16
    )
    compact_behind = pack_slots(scaled, target_behind)
    combined_behind = route_slots(compact_behind, expert_backward, shards)
    picked_behind = jnp.take(combined_behind, target_behind, axis=0)
    input_grad = grad_rows + jnp.sum(picked_behind.reshape(-1, TOP, model_width), axis=1)
    grad_handoff = from_behind(input_grad.astype(jnp.bfloat16)[None], "pipe", -1)
    return (input_handoff, grad_handoff)


def solution(mesh):
    in_specs = (
        P("pipe", "ep", None),
        P("pipe", "ep", None),
        P("pipe", "ep", None),
        P("pipe", "ep", None),
        P("pipe", "ep", None),
        P("pipe", "ep", None),
        P(None, "ep"),
        P(None, "ep"),
        P("ep", None),
        P("pipe", None, "ep"),
        P("pipe", None, "ep"),
    )
    out_specs = (P("pipe", "ep", None), P("pipe", "ep", None))
    return jax.shard_map(body, mesh=mesh, in_specs=in_specs, out_specs=out_specs, check_vma=False)
```

profile of v0, /device:TPU:192, one launch (start us, length us, event | category | flops | bytes accessed | tf_op | source)
XLA Modules:
  0.0 229.6 jit_solution(10805898320743066472)
XLA Ops:
  0.6 0.7 reduce.2
  1.3 0.1 reshape_squeeze.9
  1.4 0.2 reduce_window_sum.18
  1.6 0.8 convert_bitcast_fusion
  2.5 0.1 broadcast_in_dim.40
  2.5 0.0 copy-start.6
  2.5 0.0 copy-start.3
  2.6 0.1 reshape.82
  2.7 0.7 reduce.3
  3.4 0.1 mul.74
  3.5 0.3 convolution_convert_fusion.1
  3.7 0.1 broadcast_in_dim.41
  3.8 2.2 broadcast_in_dim.42
  6.0 10.6 %all-to-all-start.2 = ((bf16[64,2,7168]{2,1,0:T(2,128)(2,1)}), bf16[64,2,7168]{2,1,0:T(2,128)(2,1)S(1)}, u32[]{:S(2)}, u32[]{:S(2)}) async-start(bf16[64,2,7168]{2,1,0:T(2,128)(2,1)} %bitcast.43), calls=%async_computation.2 | async-start | bytes 3670016 | tf_op jit(solution)/shard_map/all_to_all | solution.py:36
  16.6 0.0 copy-done.6
  16.6 0.1 reshape_squeeze.8
  16.7 0.2 reduce_window_sum.17
  16.9 0.0 copy-done.3
  16.9 0.1 broadcast_in_dim.21
  17.1 0.2 convolution_convert_fusion.2
  17.3 0.1 broadcast_in_dim.38
  17.4 45.0 %all-to-all-done.2 = bf16[64,2,7168]{2,1,0:T(2,128)(2,1)S(1)} async-done(((bf16[64,2,7168]{2,1,0:T(2,128)(2,1)}), bf16[64,2,7168]{2,1,0:T(2,128)(2,1)S(1)}, u32[]{:S(2)}, u32[]{:S(2)}) %all-to-all-start.2) | async-done | bytes 1835040 | tf_op jit(solution)/shard_map/all_to_all | solution.py:36
  62.3 2.2 broadcast_in_dim.39
  64.5 5.6 %all-to-all-start = ((bf16[64,2,7168]{2,1,0:T(2,128)(2,1)}), bf16[64,2,7168]{2,1,0:T(2,128)(2,1)}, u32[]{:S(2)}, u32[]{:S(2)}) async-start(bf16[64,2,7168]{2,1,0:T(2,128)(2,1)} %bitcast.44), calls=%async_computation | async-start | bytes 3670016 | tf_op jit(solution)/shard_map/all_to_all | solution.py:36
  70.1 1.7 all_to_all.35
  71.8 4.1 %fusion.36 = f32[128,256]{1,0:T(8,128)S(1)} fusion(bf16[128,7168]{1,0:T(8,128)(2,1)} %all_to_all.35, bf16[256,7168]{1,0:T(8,128)(2,1)} %param.21), kind=kOutput, calls=%fused_computation.67 | convolution fusion | flops 469762048 | bytes 5636096 | tf_op jit(solution)/shard_map/dot_general | solution.py:72
  75.9 0.0 copy-done
  75.9 0.0 copy-done.2
  75.9 0.0 copy-done.5
  75.9 0.0 copy-start.1
  75.9 1.3 fusion.20
  77.2 0.7 copy-done.1
  78.0 1.3 fusion
  79.3 0.0 copy-start.7
  79.3 1.7 all_to_all.36
  81.0 34.7 %all-to-all-done = bf16[64,2,7168]{2,1,0:T(2,128)(2,1)} async-done(((bf16[64,2,7168]{2,1,0:T(2,128)(2,1)}), bf16[64,2,7168]{2,1,0:T(2,128)(2,1)}, u32[]{:S(2)}, u32[]{:S(2)}) %all-to-all-start) | async-done | bytes 1835040 | tf_op jit(solution)/shard_map/all_to_all | solution.py:36
  115.7 5.7 %all-to-all-start.3 = ((bf16[64,2,7168]{2,1,0:T(2,128)(2,1)}), bf16[64,2,7168]{2,1,0:T(2,128)(2,1)}, u32[]{:S(2)}, u32[]{:S(2)}) async-start(bf16[64,2,7168]{2,1,0:T(2,128)(2,1)} %all_to_all.36), calls=%async_computation.3 | async-start | bytes 3670016 | tf_op jit(solution)/shard_map/all_to_all | solution.py:38
  121.5 0.1 mul.69
  121.6 4.1 %all_to_all.30 = bf16[128,7168]{1,0:T(8,128)(2,1)S(1)} reshape(bf16[64,2,7168]{2,1,0:T(2,128)(2,1)} %all-to-all-done) | data formatting | bytes 3670016 | tf_op jit(solution)/shard_map/all_to_all | solution.py:36
  125.7 2.7 %fusion.35 = f32[128,256]{1,0:T(8,128)S(1)} fusion(bf16[128,7168]{1,0:T(8,128)(2,1)S(1)} %all_to_all.30, bf16[7168,256]{1,0:T(8,128)(2,1)} %param.19), kind=kOutput, calls=%fused_computation.66 | convolution fusion | flops 469762048 | bytes 5636096 | tf_op jit(solution)/shard_map/dot_general | solution.py:63
  128.4 6.6 %convolution_convert_fusion = bf16[128,7168]{1,0:T(8,128)(2,1)} fusion(bf16[256,7168]{1,0:T(8,128)(2,1)} %param.21, bf16[128,7168]{1,0:T(8,128)(2,1)S(1)} %all_to_all.30, bf16[7168,256]{1,0:T(8,128)(2,1)} %param.20, f32[128,256]{1,0:T(8,128)S(1)} %fusion.35), kind=kOutput, calls=%fused_computation.4 | convolution fusion | flops 940638208 | bytes 11141120 | tf_op jit(solution)/shard_map/dot_general | solution.py:66
  134.9 4.7 %all_to_all.31 = bf16[64,2,7168]{2,1,0:T(2,128)(2,1)} reshape(bf16[128,7168]{1,0:T(8,128)(2,1)} %convolution_convert_fusion) | data formatting | bytes 3670016 | tf_op jit(solution)/shard_map/all_to_all | solution.py:38
  139.7 27.2 %all-to-all-done.3 = bf16[64,2,7168]{2,1,0:T(2,128)(2,1)} async-done(((bf16[64,2,7168]{2,1,0:T(2,128)(2,1)}), bf16[64,2,7168]{2,1,0:T(2,128)(2,1)}, u32[]{:S(2)}, u32[]{:S(2)}) %all-to-all-start.3) | async-done | bytes 1835040 | tf_op jit(solution)/shard_map/all_to_all | solution.py:38
  166.9 5.3 %all-to-all-start.1 = ((bf16[64,2,7168]{2,1,0:T(2,128)(2,1)}), bf16[64,2,7168]{2,1,0:T(2,128)(2,1)S(1)}, u32[]{:S(2)}, u32[]{:S(2)}) async-start(bf16[64,2,7168]{2,1,0:T(2,128)(2,1)} %all_to_all.31), calls=%async_computation.1 | async-start | bytes 3670016 | tf_op jit(solution)/shard_map/all_to_all | solution.py:38
  172.2 3.3 %convert_reduce_fusion = f32[8,2,7168]{2,1,0:T(2,128)S(1)} fusion(bf16[64,2,7168]{2,1,0:T(2,128)(2,1)} %all-to-all-done.3), kind=kLoop, calls=%fused_computation.7 | loop fusion | flops 1720320 | bytes 2293760 | tf_op jit(solution)/shard_map/reduce_sum | solution.py:39
  175.5 0.0 copy-start.4
  175.5 0.3 reshape.83
  175.9 0.7 gather_fusion.1
  176.5 0.1 broadcast_select_fusion
  176.6 0.1 reshape.84
  176.8 0.2 reduce_sum.64
  177.1 1.9 collective-permute-start.1
  179.0 38.9 %all-to-all-done.1 = bf16[64,2,7168]{2,1,0:T(2,128)(2,1)S(1)} async-done(((bf16[64,2,7168]{2,1,0:T(2,128)(2,1)}), bf16[64,2,7168]{2,1,0:T(2,128)(2,1)S(1)}, u32[]{:S(2)}, u32[]{:S(2)}) %all-to-all-start.1) | async-done | bytes 1835040 | tf_op jit(solution)/shard_map/all_to_all | solution.py:38
  217.9 1.6 convert_reduce_fusion.1
  219.5 0.3 reshape.80
  219.8 0.7 gather_fusion
  220.5 0.1 select_multiply_fusion
  220.6 0.1 reshape.81
  220.7 0.2 reduce_sum.60
  221.0 5.5 %collective-permute-start = (bf16[1,3,7168]{2,1,0:T(4,128)(2,1)S(1)}, bf16[1,3,7168]{2,1,0:T(4,128)(2,1)S(1)}, u32[]{:S(2)}, u32[]{:S(2)}) collective-permute-start(bf16[1,3,7168]{2,1,0:T(4,128)(2,1)S(1)} %fusion.18), channel_id=1, source_target_pairs={{0,64},{64,128},{128,192},{192,256},{256,320},{320,384},{384,448},... | collective-permute-start | bytes 129032 | tf_op jit(solution)/shard_map/ppermute | solution.py:14
  226.5 0.0 collective-permute-done.1
  226.5 1.8 collective-permute-done
  228.3 0.6 copy.15
  229.0 0.6 copy.16
  (20 shorter events, 0.3 us)
Async XLA Ops:
  2.5 14.1 %copy-start.6 = (s32[1,3,4]{2,0,1:T(1,128)S(1)}, s32[1,3,4]{2,0,1:T(1,128)}, u32[]{:S(2)}) copy-start(s32[1,3,4]{2,0,1:T(1,128)} %param.15) | copy-start | bytes 148
  2.5 14.4 %copy-start.3 = (bf16[1,3,7168]{2,1,0:T(4,128)(2,1)S(1)}, bf16[1,3,7168]{2,1,0:T(4,128)(2,1)}, u32[]{:S(2)}) copy-start(bf16[1,3,7168]{2,1,0:T(4,128)(2,1)} %param.13) | copy-start | bytes 129028
  6.0 56.3 %all-to-all-start.2 = ((bf16[64,2,7168]{2,1,0:T(2,128)(2,1)}), bf16[64,2,7168]{2,1,0:T(2,128)(2,1)S(1)}, u32[]{:S(2)}, u32[]{:S(2)}) async-start(bf16[64,2,7168]{2,1,0:T(2,128)(2,1)} %bitcast.43), calls=%async_computation.2 | async-start | bytes 3670016 | tf_op jit(solution)/shard_map/all_to_all | solution.py:36
  64.5 51.2 %all-to-all-start = ((bf16[64,2,7168]{2,1,0:T(2,128)(2,1)}), bf16[64,2,7168]{2,1,0:T(2,128)(2,1)}, u32[]{:S(2)}, u32[]{:S(2)}) async-start(bf16[64,2,7168]{2,1,0:T(2,128)(2,1)} %bitcast.44), calls=%async_computation | async-start | bytes 3670016 | tf_op jit(solution)/shard_map/all_to_all | solution.py:36
  71.8 4.1 %copy-start = (bf16[7168,256]{1,0:T(8,128)(2,1)S(1)}, bf16[7168,256]{1,0:T(8,128)(2,1)}, u32[]{:S(2)}) copy-start(bf16[7168,256]{1,0:T(8,128)(2,1)} %param.19) | copy-start | bytes 11010052
  71.8 4.1 %copy-start.2 = (bf16[1,128,256]{2,1,0:T(8,128)(2,1)S(1)}, bf16[1,128,256]{2,1,0:T(8,128)(2,1)}, u32[]{:S(2)}) copy-start(bf16[1,128,256]{2,1,0:T(8,128)(2,1)} %param.22) | copy-start | bytes 196612
  71.8 4.1 %copy-start.5 = (bf16[1,128,256]{2,1,0:T(8,128)(2,1)S(1)}, bf16[1,128,256]{2,1,0:T(8,128)(2,1)}, u32[]{:S(2)}) copy-start(bf16[1,128,256]{2,1,0:T(8,128)(2,1)} %param.23) | copy-start | bytes 196612
  75.9 2.0 copy-start.1
  79.3 42.1 %copy-start.7 = (f32[1,3,4]{2,0,1:T(1,128)S(1)}, f32[1,3,4]{2,0,1:T(1,128)}, u32[]{:S(2)}) copy-start(f32[1,3,4]{2,0,1:T(1,128)} %param.16) | copy-start | bytes 148
  115.7 51.2 %all-to-all-start.3 = ((bf16[64,2,7168]{2,1,0:T(2,128)(2,1)}), bf16[64,2,7168]{2,1,0:T(2,128)(2,1)}, u32[]{:S(2)}, u32[]{:S(2)}) async-start(bf16[64,2,7168]{2,1,0:T(2,128)(2,1)} %all_to_all.36), calls=%async_computation.3 | async-start | bytes 3670016 | tf_op jit(solution)/shard_map/all_to_all | solution.py:38
  166.9 51.1 %all-to-all-start.1 = ((bf16[64,2,7168]{2,1,0:T(2,128)(2,1)}), bf16[64,2,7168]{2,1,0:T(2,128)(2,1)S(1)}, u32[]{:S(2)}, u32[]{:S(2)}) async-start(bf16[64,2,7168]{2,1,0:T(2,128)(2,1)} %all_to_all.31), calls=%async_computation.1 | async-start | bytes 3670016 | tf_op jit(solution)/shard_map/all_to_all | solution.py:38
  175.5 1.5 copy-start.4
  177.1 49.5 %collective-permute-start.1 = (bf16[1,3,7168]{2,1,0:T(4,128)(2,1)S(1)}, bf16[1,3,7168]{2,1,0:T(4,128)(2,1)S(1)}, u32[]{:S(2)}, u32[]{:S(2)}) collective-permute-start(bf16[1,3,7168]{2,1,0:T(4,128)(2,1)S(1)} %fusion.17), channel_id=1, source_target_pairs={{64,0},{128,64},{192,128},{256,192},{320,256},{384,320},{448,384},... | collective-permute-start | bytes 129032 | tf_op jit(solution)/shard_map/ppermute | solution.py:14
  221.0 7.3 %collective-permute-start = (bf16[1,3,7168]{2,1,0:T(4,128)(2,1)S(1)}, bf16[1,3,7168]{2,1,0:T(4,128)(2,1)S(1)}, u32[]{:S(2)}, u32[]{:S(2)}) collective-permute-start(bf16[1,3,7168]{2,1,0:T(4,128)(2,1)S(1)} %fusion.18), channel_id=1, source_target_pairs={{0,64},{64,128},{128,192},{192,256},{256,320},{320,384},{384,448},... | collective-permute-start | bytes 129032 | tf_op jit(solution)/shard_map/ppermute | solution.py:14
where the time goes:
time: 230 us
  waiting for transfers between devices  148 us (64%)
  starting transfers between devices  34.6 us (15%)
  local copies, waits for them, and re-layouts  21.6 us (9%)
  matrix products  16.4 us (7%)
  other arithmetic  8.37 us (4%)
    all_to_all x2, waiting for transfers between devices, route_slots(): lax.all_to_all(spread_rows, 'ep', split_axis=0, concat_axis=0, tiled=True)  79.7 us
    all_to_all x2, waiting for transfers between devices, route_slots(): lax.all_to_all(results, 'ep', split_axis=0, concat_axis=0, tiled=True)  66.1 us
    all_to_all x2, starting transfers between devices, route_slots(): lax.all_to_all(spread_rows, 'ep', split_axis=0, concat_axis=0, tiled=True)  16.1 us
    all_to_all x2, starting transfers between devices, route_slots(): lax.all_to_all(results, 'ep', split_axis=0, concat_axis=0, tiled=True)  11.1 us
    ppermute x2, starting transfers between devices, from_behind(): return lax.ppermute(shard, axis, pairs)  7.41 us
    dot_general x1, matrix products, expert_forward(): jnp.dot(hidden, down_weight, preferred_element_type=jnp.float32)  6.58 us
    all_to_all x2, local copies, waits for them, and re-layouts, route_slots(): lax.all_to_all(results, 'ep', split_axis=0, concat_axis=0, tiled=True)  6.43 us
    all_to_all x2, local copies, waits for them, and re-layouts, route_slots(): lax.all_to_all(spread_rows, 'ep', split_axis=0, concat_axis=0, tiled=True)  5.76 us
  transfers between devices with their start and end apart: 6, of which 5 were waited for; matrix products, arithmetic and copies ran while one was open for 11% of the time, Pallas kernels for 0%

commit v1 on v0

v1 whole, which is shorter than its diff:
```python
import functools

import jax
import jax.numpy as jnp
from jax import lax
from jax.experimental import pallas as pl
from jax.experimental.pallas import tpu as pltpu
from jax.sharding import PartitionSpec as P

EXPERTS = 8
TOP = 4
CAP = 2
TOK = 3
CORES = 2
RING = 4
CHUNKS = 4
MESH = pl.DeviceIdType.MESH
LAST = (((1,), (1,)), ((), ()))


def kernel(
    cuts,
    act_hbm,
    cot_hbm,
    fexp,
    fwt,
    bexp,
    bwt,
    wg_hbm,
    wu_hbm,
    wd_hbm,
    sg_hbm,
    su_hbm,
    out_f,
    out_b,
    tok,
    wg,
    wu,
    wd,
    sg,
    su,
    ysend,
    yrecv,
    rows,
    gacc,
    uacc,
    hacc,
    hid,
    ggrad,
    ugrad,
    psend,
    precv,
    pown,
    t2s,
    t2r,
    ts,
    tr,
    hs,
    hr,
    osend,
    in_sem,
    y_ss,
    y_rs,
    x_ss,
    x_rs,
    r_ss,
    r_rs,
    h_ss,
    h_rs,
    z_ss,
    z_rs,
):
    sections = lax.axis_size("pipe")
    section = lax.axis_index("pipe")
    place = lax.axis_index("ep")
    y = place // (RING * CORES)
    x = (place // CORES) % RING
    c = place % CORES
    width = tok.shape[2]
    wide = width // cuts
    half = wide // 2
    block = EXPERTS * CAP
    side = RING * block
    outs = (out_f, out_b)

    def at(yy, xx, cc):
        return (section, (yy * RING + xx) * CORES + cc)

    right = at(y, (x + 1) % RING, c)
    left = at(y, (x + RING - 1) % RING, c)
    partner = at(y, x, 1 - c)

    def expert_of(d):
        return at((y + EXPERTS - d) % EXPERTS, x, c)

    def source_of(d):
        return at((y + d) % EXPERTS, x, c)

    def cols(ch):
        return pl.ds(ch * wide, wide)

    def remote(src, dst, ss, rs, dev):
        return pltpu.make_async_remote_copy(
            src_ref=src, dst_ref=dst, send_sem=ss, recv_sem=rs, device_id=dev, device_id_type=MESH
        )

    loads = {}

    def load(name, src, dst, number):
        copy = pltpu.make_async_copy(src, dst, in_sem.at[number])
        copy.start()
        loads[name] = copy

    def need(name):
        copy = loads.pop(name, None)
        if copy is not None:
            copy.wait()

    load("act", act_hbm.at[0], tok.at[0], 0)
    load("cot", cot_hbm.at[0], tok.at[1], 1)
    load("wg", wg_hbm, wg, 2)
    load("wu", wu_hbm, wu, 3)
    load("wd", wd_hbm, wd, 4)
    load("sg", sg_hbm.at[0], sg, 5)
    load("su", su_hbm.at[0], su, 6)

    barrier = pltpu.get_barrier_semaphore()

    def greet(dev):
        pl.semaphore_signal(barrier, inc=1, device_id=dev, device_id_type=MESH)

    for d in range(1, EXPERTS):
        greet(expert_of(d))
    greet(right)
    greet(left)
    greet(partner)

    @pl.when(section + 1 < sections)
    def _():
        greet((section + 1, place))

    @pl.when(section > 0)
    def _():
        greet((section - 1, place))

    shape = (EXPERTS, CAP, 128)
    far = lax.broadcasted_iota(jnp.int32, shape, 0)
    which = lax.broadcasted_iota(jnp.int32, shape, 1)
    expert = (y + EXPERTS - far) & (EXPERTS - 1)

    def tables(ids, weights):
        seen = jnp.zeros(shape, jnp.int32)
        plain, weighted = [], []
        for t in range(TOK):
            has = jnp.zeros(shape, jnp.int32)
            weight = jnp.zeros(shape, jnp.float32)
            for k in range(ids.shape[2]):
                hit = expert == ids[0, t, k]
                has = jnp.where(hit, 1, has)
                weight = jnp.where(hit, weights[0, t, k], weight)
            here = jnp.where(seen == which, has, 0)
            plain.append(jnp.where(here == 1, 1.0, 0.0).astype(jnp.float32))
            weighted.append(jnp.where(here == 1, weight, 0.0))
            seen = seen + has
        return plain, weighted

    plain_f, weighted_f = tables(fexp, fwt)
    plain_b, weighted_b = tables(bexp, bwt)
    pack_table = (plain_f, weighted_b)
    join_table = (weighted_f, plain_b)

    copies = {}

    def pack(st, ch):
        values = tok[st, :, cols(ch)].astype(jnp.float32)
        for d in range(EXPERTS):
            total = None
            for t in range(TOK):
                term = pack_table[st][t][d][:, 0:1] * values[t : t + 1, :]
                total = term if total is None else total + term
            if d == 0:
                yrecv[st, ch, 0] = total.astype(jnp.bfloat16)
            else:
                ysend[st, ch, d] = total.astype(jnp.bfloat16)

    def send_slots(st, ch):
        for d in range(1, EXPERTS):
            copy = remote(
                ysend.at[st, ch, d],
                yrecv.at[st, ch, d],
                y_ss.at[st, ch, d],
                y_rs.at[st, ch, d],
                expert_of(d),
            )
            copy.start()
            copies["y", st, ch, d] = copy

    def spread(name, st, ch, number, src, dst, dev):
        copy = remote(src, dst, x_ss.at[st, ch, number], x_rs.at[st, ch, number], dev)
        copy.start()
        copies[name, st, ch] = copy

    def part(st, ch, gamma, delta):
        return rows.at[st, ch, pl.ds((gamma * RING + delta) * block, block), :]

    def halfpart(st, ch, gamma, delta, number):
        return rows.at[
            st, ch, pl.ds((gamma * RING + delta) * block, block), pl.ds(number * half, half)
        ]

    def stage_a(st, ch):
        for d in range(1, EXPERTS):
            copies["y", st, ch, d].wait_recv()
        own = yrecv[st, ch].astype(jnp.float32).reshape(block, wide)
        rows[st, ch, 0:block, :] = own.astype(jnp.bfloat16)
        spread("xr", st, ch, 0, part(st, ch, 0, 0), part(st, ch, 0, 3), right)
        spread("xl", st, ch, 1, part(st, ch, 0, 0), part(st, ch, 0, 1), left)
        spread("c0", st, ch, 2, part(st, ch, 0, 0), part(st, ch, 1, 0), partner)

    def stage_b(st, ch):
        copies["xl", st, ch].wait_recv()
        spread("hl", st, ch, 3, halfpart(st, ch, 0, 1, 0), halfpart(st, ch, 0, 2, 0), left)
        copies["xr", st, ch].wait_recv()
        spread("hr", st, ch, 4, halfpart(st, ch, 0, 3, 1), halfpart(st, ch, 0, 2, 1), right)
        spread("c1", st, ch, 5, part(st, ch, 0, 1), part(st, ch, 1, 1), partner)
        spread("c3", st, ch, 6, part(st, ch, 0, 3), part(st, ch, 1, 3), partner)

    def stage_c(st, ch):
        copies["hl", st, ch].wait_recv()
        copies["hr", st, ch].wait_recv()
        spread("c2", st, ch, 7, part(st, ch, 0, 2), part(st, ch, 1, 2), partner)

    def stage_d(st, ch):
        for name in ("c0", "c1", "c3", "c2"):
            copies[name, st, ch].wait_recv()
        arrived = rows[st, ch]
        if st == 0:
            if ch == 0:
                need("wg")
                need("wu")
            gate = jnp.dot(arrived, wg[cols(ch), :], preferred_element_type=jnp.float32)
            up = jnp.dot(arrived, wu[cols(ch), :], preferred_element_type=jnp.float32)
            if ch == 0:
                gacc[...] = gate
                uacc[...] = up
            else:
                gacc[...] += gate
                uacc[...] += up
        else:
            if ch == 0:
                need("wd")
            grad = lax.dot_general(arrived, wd[:, cols(ch)], LAST, preferred_element_type=jnp.float32)
            if ch == 0:
                hacc[...] = grad
            else:
                hacc[...] += grad

    def middle(st):
        if st == 0:
            gate = gacc[...]
            hid[...] = (gate * jax.nn.sigmoid(gate) * uacc[...]).astype(jnp.bfloat16)
        else:
            grad = hacc[...]
            need("sg")
            need("su")
            count = 2 * side
            mine = lax.broadcasted_iota(jnp.int32, (count, count), 0)
            theirs = lax.broadcasted_iota(jnp.int32, (count, count), 1)
            j = mine % CAP
            d = (mine // CAP) % EXPERTS
            delta = (mine // block) % RING
            gamma = mine // side
            ys = (y + d) % EXPERTS
            xs = (x + delta) % RING
            cs = (c + gamma) % CORES
            wanted = ((ys * RING + xs) * CORES + cs) * CAP + j
            order = jnp.where(wanted == theirs, 1.0, 0.0).astype(jnp.bfloat16)
            gate = jnp.dot(order, sg[...], preferred_element_type=jnp.float32)
            up = jnp.dot(order, su[...], preferred_element_type=jnp.float32)
            sig = jax.nn.sigmoid(gate)
            ggrad[...] = (grad * up * sig * (1.0 + gate * (1.0 - sig))).astype(jnp.bfloat16)
            ugrad[...] = (grad * (gate * sig)).astype(jnp.bfloat16)

    def back(name, st, ch, number, src, dst, dev):
        copy = remote(src, dst, r_ss.at[st, ch, number], r_rs.at[st, ch, number], dev)
        copy.start()
        copies[name, st, ch] = copy

    def stage_e(st, ch):
        if st == 0:
            if ch == 0:
                need("wd")
            partial = jnp.dot(hid[...], wd[:, cols(ch)], preferred_element_type=jnp.float32)
        else:
            partial = lax.dot_general(
                ggrad[...], wg[cols(ch), :], LAST, preferred_element_type=jnp.float32
            )
            partial = partial + lax.dot_general(
                ugrad[...], wu[cols(ch), :], LAST, preferred_element_type=jnp.float32
            )
        psend[st, ch] = partial[side:, :].astype(jnp.bfloat16)
        back("p", st, ch, 0, psend.at[st, ch], precv.at[st, ch], partner)
        pown[st, ch] = partial[:side, :]

    def stage_f(st, ch):
        copies["p", st, ch].wait_recv()
        far_rows = pl.ds(2 * block, block)
        t2s[st, ch] = (
            pown[st, ch, far_rows, :] + precv[st, ch, far_rows, :].astype(jnp.float32)
        ).astype(jnp.bfloat16)
        a, b = pl.ds(0, half), pl.ds(half, half)
        back("tl", st, ch, 1, t2s.at[st, ch, :, a], t2r.at[st, ch, :, a], left)
        back("tr", st, ch, 2, t2s.at[st, ch, :, b], t2r.at[st, ch, :, b], right)

    def chip_sum(st, ch, delta):
        some = pl.ds(delta * block, block)
        return pown[st, ch, some, :] + precv[st, ch, some, :].astype(jnp.float32)

    def stage_g(st, ch):
        to_left = chip_sum(st, ch, 3)
        copies["tl", st, ch].wait_recv()
        ts[st, ch, 0, :, 0:half] = (
            to_left[:, :half] + t2r[st, ch, :, 0:half].astype(jnp.float32)
        ).astype(jnp.bfloat16)
        ts[st, ch, 0, :, half:wide] = to_left[:, half:].astype(jnp.bfloat16)
        back("sl", st, ch, 3, ts.at[st, ch, 0], tr.at[st, ch, 0], left)
        to_right = chip_sum(st, ch, 1)
        copies["tr", st, ch].wait_recv()
        ts[st, ch, 1, :, 0:half] = to_right[:, :half].astype(jnp.bfloat16)
        ts[st, ch, 1, :, half:wide] = (
            to_right[:, half:] + t2r[st, ch, :, half:wide].astype(jnp.float32)
        ).astype(jnp.bfloat16)
        back("sr", st, ch, 4, ts.at[st, ch, 1], tr.at[st, ch, 1], right)

    def stage_h(st, ch):
        own = chip_sum(st, ch, 0)
        copies["sl", st, ch].wait_recv()
        copies["sr", st, ch].wait_recv()
        own = own + tr[st, ch, 0].astype(jnp.float32) + tr[st, ch, 1].astype(jnp.float32)
        for d in range(EXPERTS):
            piece = own[d * CAP : (d + 1) * CAP, :].astype(jnp.bfloat16)
            if d == 0:
                hr[st, ch, 0] = piece
            else:
                hs[st, ch, d] = piece
        for d in range(1, EXPERTS):
            copy = remote(
                hs.at[st, ch, d],
                hr.at[st, ch, d],
                h_ss.at[st, ch, d],
                h_rs.at[st, ch, d],
                source_of(d),
            )
            copy.start()
            copies["h", st, ch, d] = copy

    def handoff(st, ch):
        to = section + 1 if st == 0 else section - 1
        return remote(
            osend.at[st, ch],
            outs[st].at[0, :, cols(ch)],
            z_ss.at[st, ch],
            z_rs.at[st, ch],
            (to, place),
        )

    def gives(st):
        return section + 1 < sections if st == 0 else section > 0

    def takes(st):
        return section > 0 if st == 0 else section + 1 < sections

    def stage_i(st, ch):
        for d in range(1, EXPERTS):
            copies["h", st, ch, d].wait_recv()
        base = tok[st, :, cols(ch)].astype(jnp.float32)
        lines = []
        for t in range(TOK):
            total = None
            for d in range(EXPERTS):
                term = join_table[st][t][d][:, 0:1] * hr[st, ch, d].astype(jnp.float32)
                total = term if total is None else total + term
            lines.append(base[t : t + 1, :] + total[0:1, :] + total[1:2, :])
        osend[st, ch] = jnp.concatenate(lines, axis=0).astype(jnp.bfloat16)

        @pl.when(gives(st))
        def _():
            handoff(st, ch).start()

    chunks = [(st, ch) for st in range(2) for ch in range(cuts)]
    need("act")
    for ch in range(cuts):
        pack(0, ch)
    ends = (section + 1 < sections).astype(jnp.int32) + (section > 0).astype(jnp.int32)
    pl.semaphore_wait(barrier, EXPERTS - 1 + 3 + ends)

    for ch in range(cuts):
        send_slots(0, ch)
    need("cot")
    for ch in range(cuts):
        pack(1, ch)
        send_slots(1, ch)

    stages = (
        (stage_a, 0),
        (stage_b, 1),
        (stage_c, 2),
        (stage_d, 3),
        (stage_e, cuts + 3),
        (stage_f, cuts + 4),
        (stage_g, cuts + 5),
        (stage_h, cuts + 6),
        (stage_i, cuts + 8),
    )
    total_steps = len(chunks) + stages[-1][1]
    for step in range(total_steps):
        for stage, lag in stages:
            number = step - lag
            if 0 <= number < len(chunks):
                st, ch = chunks[number]
                stage(st, ch)
                if stage is stage_d and ch == cuts - 1:
                    middle(st)

    for st in range(2):

        @pl.when(takes(st))
        def _():
            for ch in range(cuts):
                handoff(st, ch).wait_recv()

        @pl.when(jnp.logical_not(takes(st)))
        def _():
            outs[st][...] = jnp.zeros_like(outs[st])

        @pl.when(gives(st))
        def _():
            for ch in range(cuts):
                handoff(st, ch).wait_send()

    for copy in copies.values():
        copy.wait_send()


def body(
    activations,
    cotangent,
    forward_experts,
    forward_weights,
    backward_experts,
    backward_weights,
    gate_weight,
    up_weight,
    down_weight,
    saved_gate,
    saved_up,
):
    cuts = CHUNKS
    tokens, width = activations.shape[1:]
    units = gate_weight.shape[1]
    slots = saved_gate.shape[1]
    wide = width // cuts
    block = EXPERTS * CAP
    side = RING * block
    anywhere = pl.BlockSpec(memory_space=pl.ANY)
    scalar = pl.BlockSpec(memory_space=pltpu.SMEM)
    vmem = pl.BlockSpec(memory_space=pltpu.VMEM)
    half = jnp.bfloat16
    full = jnp.float32
    dma = pltpu.SemaphoreType.DMA
    out = jax.ShapeDtypeStruct(activations.shape, half)
    return pl.pallas_call(
        functools.partial(kernel, cuts),
        out_shape=(out, out),
        in_specs=[anywhere, anywhere, scalar, scalar, scalar, scalar] + [anywhere] * 5,
        out_specs=(vmem, vmem),
        scratch_shapes=[
            pltpu.VMEM((2, tokens, width), half),
            pltpu.VMEM((width, units), half),
            pltpu.VMEM((width, units), half),
            pltpu.VMEM((units, width), half),
            pltpu.VMEM((slots, units), half),
            pltpu.VMEM((slots, units), half),
            pltpu.VMEM((2, cuts, EXPERTS, CAP, wide), half),
            pltpu.VMEM((2, cuts, EXPERTS, CAP, wide), half),
            pltpu.VMEM((2, cuts, slots, wide), half),
            pltpu.VMEM((slots, units), full),
            pltpu.VMEM((slots, units), full),
            pltpu.VMEM((slots, units), full),
            pltpu.VMEM((slots, units), half),
            pltpu.VMEM((slots, units), half),
            pltpu.VMEM((slots, units), half),
            pltpu.VMEM((2, cuts, side, wide), half),
            pltpu.VMEM((2, cuts, side, wide), half),
            pltpu.VMEM((2, cuts, side, wide), full),
            pltpu.VMEM((2, cuts, block, wide), half),
            pltpu.VMEM((2, cuts, block, wide), half),
            pltpu.VMEM((2, cuts, 2, block, wide), half),
            pltpu.VMEM((2, cuts, 2, block, wide), half),
            pltpu.VMEM((2, cuts, EXPERTS, CAP, wide), half),
            pltpu.VMEM((2, cuts, EXPERTS, CAP, wide), half),
            pltpu.VMEM((2, cuts, tokens, wide), half),
            dma((7,)),
            dma((2, cuts, EXPERTS)),
            dma((2, cuts, EXPERTS)),
            dma((2, cuts, 8)),
            dma((2, cuts, 8)),
            dma((2, cuts, 5)),
            dma((2, cuts, 5)),
            dma((2, cuts, EXPERTS)),
            dma((2, cuts, EXPERTS)),
            dma((2, cuts)),
            dma((2, cuts)),
        ],
        compiler_params=pltpu.CompilerParams(
            collective_id=0, has_side_effects=True, vmem_limit_bytes=60 * 1024 * 1024
        ),
    )(
        activations,
        cotangent,
        forward_experts,
        forward_weights,
        backward_experts,
        backward_weights,
        gate_weight,
        up_weight,
        down_weight,
        saved_gate,
        saved_up,
    )


def solution(mesh):
    in_specs = (
        P("pipe", "ep", None),
        P("pipe", "ep", None),
        P("pipe", "ep", None),
        P("pipe", "ep", None),
        P("pipe", "ep", None),
        P("pipe", "ep", None),
        P(None, "ep"),
        P(None, "ep"),
        P("ep", None),
        P("pipe", None, "ep"),
        P("pipe", None, "ep"),
    )
    out_specs = (P("pipe", "ep", None), P("pipe", "ep", None))
    return jax.shard_map(body, mesh=mesh, in_specs=in_specs, out_specs=out_specs, check_vma=False)
```

time: 230 us -> 87.3 us (0.38)
  waiting for transfers between devices: 148 us -> 0 us
  Pallas kernels: 0 us -> 78.3 us
  starting transfers between devices: 34.6 us -> 0 us
  matrix products: 16.4 us -> 0 us
  local copies, waits for them, and re-layouts: 21.6 us -> 7.96 us
  other arithmetic: 8.37 us -> 0 us
    all_to_all x4 -> x0, waiting for transfers between devices: 146 us -> none  [the longest x2 79.7 us: route_slots(): lax.all_to_all(spread_rows, 'ep', split_axis=0, concat_axis=0, tiled=True)]
    pallas_call x0 -> x1, Pallas kernels: none -> 78.3 us  [body(): pl.pallas_call(functools.partial(kernel, cuts), out_shape=(out, out), in_...]
    all_to_all x4 -> x0, starting transfers between devices: 27.2 us -> none  [the longest x2 16.1 us: route_slots(): lax.all_to_all(spread_rows, 'ep', split_axis=0, concat_axis=0, tiled=True)]
    dot_general x7 -> x0, matrix products: 16.4 us -> none  [the longest x1 6.58 us: expert_forward(): jnp.dot(hidden, down_weight, preferred_element_type=jnp.float32)]
    all_to_all x4 -> x0, local copies, waits for them, and re-layouts: 12.2 us -> none  [the longest x2 6.43 us: route_slots(): lax.all_to_all(results, 'ep', split_axis=0, concat_axis=0, tiled=True)]
    ppermute x2 -> x0, starting transfers between devices: 7.41 us -> none  [from_behind(): return lax.ppermute(shard, axis, pairs)]
    unnamed x18 -> x6, local copies, waits for them, and re-layouts: 2 us -> 7.96 us
    reduce_sum x6 -> x0, other arithmetic: 5.43 us -> none  [the longest x2 4.91 us: route_slots(): jnp.sum(returned.astype(jnp.float32).reshape(EXPERTS, shards, CAP, model_...]
  transfers between devices with their start and end apart: 6 -> 0, of which waited for: 5 -> 0; matrix products, arithmetic and copies ran while one was open for 11% -> 0% of each run, Pallas kernels for 0% -> 0%
where the time goes in v1:
time: 87.3 us; the launch traced here: 86.9 us
  Pallas kernels  78.3 us (90%)
  local copies, waits for them, and re-layouts  7.96 us (9%)
    pallas_call x1, Pallas kernels, body(): pl.pallas_call(functools.partial(kernel, cuts), out_shape=(out, out), in_...  78.3 us
    unnamed x6, local copies, waits for them, and re-layouts  7.96 us

profile of v1, /device:TPU:192, one launch (start us, length us, event | category | flops | bytes accessed | tf_op | source)
XLA Modules:
  0.0 86.9 jit_solution(2137304470682950792)
XLA Ops:
  0.6 1.3 %copy.13.fexp = s32[1,3,4]{2,1,0:T(4,128)} copy(s32[1,3,4]{2,0,1:T(1,128)} %param.13) | data formatting | bytes 96 | tf_op args[2]
  1.9 1.3 %copy.14.fwt = f32[1,3,4]{2,1,0:T(4,128)} copy(f32[1,3,4]{2,0,1:T(1,128)} %param.14) | data formatting | bytes 96 | tf_op args[3]
  3.1 1.3 %copy.15.bexp = s32[1,3,4]{2,1,0:T(4,128)} copy(s32[1,3,4]{2,0,1:T(1,128)} %param.15) | data formatting | bytes 96 | tf_op args[4]
  4.4 1.2 %copy.16.bwt = f32[1,3,4]{2,1,0:T(4,128)} copy(f32[1,3,4]{2,0,1:T(1,128)} %param.16) | data formatting | bytes 96 | tf_op args[5]
  5.7 78.3 %shard_map.122 = (bf16[1,3,7168]{2,1,0:T(4,128)(2,1)}, bf16[1,3,7168]{2,1,0:T(4,128)(2,1)}) custom-call(bf16[1,3,7168]{2,1,0:T(4,128)(2,1)} %act_hbm.1, bf16[1,3,7168]{2,1,0:T(4,128)(2,1)} %cot_hbm.1, s32[1,3,4]{2,1,0:T(4,128)} %copy.13.fexp, f32[1,3,4]{2,1,0:T(4,128)} %copy.14.fwt, s32[1,3,4]{2,1,0:T(4,128)} %copy.15.bexp, f32[1,3,4]{2,1,0:T(4,128)} %copy.16.bwt, ...), custom_call_target="tpu_custom_call" | custom-call | tf_op jit(solution)/shard_map/pallas_call | solution.py:472
  84.0 1.5 %copy.19 = bf16[1,3,7168]{2,1,0:T(4,128)(2,1)} copy(bf16[1,3,7168]{2,1,0:T(4,128)(2,1)} %get-tuple-element.4) | data formatting | bytes 86016
  85.4 1.5 %copy.20 = bf16[1,3,7168]{2,1,0:T(4,128)(2,1)} copy(bf16[1,3,7168]{2,1,0:T(4,128)(2,1)} %get-tuple-element.5) | data formatting | bytes 86016

commit v2 on v1

--- a/solution.py
+++ b/solution.py
@@ -13,13 +13,23 @@
 TOK = 3
 CORES = 2
 RING = 4
-CHUNKS = 4
+WIDTHS = ((1792, 1792, 1792, 1792), (1792, 1792, 1792, 1792))
+ORDER = (
+    "P00", "P01", "P02", "P03", "P10", "P11", "P12", "P13", "A00", "A01", "A02", "B00",
+    "A03", "B01", "A10", "B02", "C00", "A11", "B03", "D00", "C01", "A12", "B10", "D01",
+    "C02", "A13", "B11", "D02", "C03", "B12", "D03", "M00", "C10", "E00", "E01", "B13",
+    "E02", "C11", "E03", "C12", "F00", "D10", "F01", "C13", "F02", "D11", "G00", "F03",
+    "G01", "D12", "D13", "M10", "G02", "E10", "E11", "H00", "E12", "G03", "E13", "F10",
+    "H01", "F11", "H02", "F12", "F13", "H03", "G10", "G11", "I00", "G12", "G13", "I01",
+    "H10", "I02", "H11", "H12", "I03", "H13", "I10", "I11", "I12", "I13",
+)
 MESH = pl.DeviceIdType.MESH
 LAST = (((1,), (1,)), ((), ()))
 
 
 def kernel(
-    cuts,
+    widths,
+    order,
     act_hbm,
     cot_hbm,
     fexp,
@@ -76,9 +86,6 @@
     y = place // (RING * CORES)
     x = (place // CORES) % RING
     c = place % CORES
-    width = tok.shape[2]
-    wide = width // cuts
-    half = wide // 2
     block = EXPERTS * CAP
     side = RING * block
     outs = (out_f, out_b)
@@ -96,8 +103,23 @@
     def source_of(d):
         return at((y + d) % EXPERTS, x, c)
 
-    def cols(ch):
-        return pl.ds(ch * wide, wide)
+    def wide(st, ch):
+        return widths[st][ch]
+
+    def split(st, ch):
+        return widths[st][ch] // 256 * 128
+
+    def start_of(st, ch):
+        return sum(widths[st][:ch])
+
+    def cols(st, ch):
+        return pl.ds(start_of(st, ch), wide(st, ch))
+
+    def low(st, ch):
+        return pl.ds(start_of(st, ch), split(st, ch))
+
+    def high(st, ch):
+        return pl.ds(start_of(st, ch) + split(st, ch), wide(st, ch) - split(st, ch))
 
     def remote(src, dst, ss, rs, dev):
         return pltpu.make_async_remote_copy(
@@ -155,9 +177,9 @@
             has = jnp.zeros(shape, jnp.int32)
             weight = jnp.zeros(shape, jnp.float32)
             for k in range(ids.shape[2]):
-                hit = expert == ids[0, t, k]
+                hit = expert == ids[t, 0, k]
                 has = jnp.where(hit, 1, has)
-                weight = jnp.where(hit, weights[0, t, k], weight)
+                weight = jnp.where(hit, weights[t, 0, k], weight)
             here = jnp.where(seen == which, has, 0)
             plain.append(jnp.where(here == 1, 1.0, 0.0).astype(jnp.float32))
             weighted.append(jnp.where(here == 1, weight, 0.0))
@@ -172,22 +194,22 @@
     copies = {}
 
     def pack(st, ch):
-        values = tok[st, :, cols(ch)].astype(jnp.float32)
+        values = tok[st, :, cols(st, ch)].astype(jnp.float32)
         for d in range(EXPERTS):
             total = None
             for t in range(TOK):
                 term = pack_table[st][t][d][:, 0:1] * values[t : t + 1, :]
                 total = term if total is None else total + term
             if d == 0:
-                yrecv[st, ch, 0] = total.astype(jnp.bfloat16)
+                yrecv[st, 0, :, cols(st, ch)] = total.astype(jnp.bfloat16)
             else:
-                ysend[st, ch, d] = total.astype(jnp.bfloat16)
+                ysend[st, d, :, cols(st, ch)] = total.astype(jnp.bfloat16)
 
     def send_slots(st, ch):
         for d in range(1, EXPERTS):
             copy = remote(
-                ysend.at[st, ch, d],
-                yrecv.at[st, ch, d],
+                ysend.at[st, d, :, cols(st, ch)],
+                yrecv.at[st, d, :, cols(st, ch)],
                 y_ss.at[st, ch, d],
                 y_rs.at[st, ch, d],
                 expert_of(d),
@@ -201,18 +223,17 @@
         copies[name, st, ch] = copy
 
     def part(st, ch, gamma, delta):
-        return rows.at[st, ch, pl.ds((gamma * RING + delta) * block, block), :]
+        return rows.at[st, pl.ds((gamma * RING + delta) * block, block), cols(st, ch)]
 
     def halfpart(st, ch, gamma, delta, number):
-        return rows.at[
-            st, ch, pl.ds((gamma * RING + delta) * block, block), pl.ds(number * half, half)
-        ]
+        some = low(st, ch) if number == 0 else high(st, ch)
+        return rows.at[st, pl.ds((gamma * RING + delta) * block, block), some]
 
     def stage_a(st, ch):
         for d in range(1, EXPERTS):
             copies["y", st, ch, d].wait_recv()
-        own = yrecv[st, ch].astype(jnp.float32).reshape(block, wide)
-        rows[st, ch, 0:block, :] = own.astype(jnp.bfloat16)
+        own = yrecv[st, :, :, cols(st, ch)].astype(jnp.float32).reshape(block, wide(st, ch))
+        rows[st, 0:block, cols(st, ch)] = own.astype(jnp.bfloat16)
         spread("xr", st, ch, 0, part(st, ch, 0, 0), part(st, ch, 0, 3), right)
         spread("xl", st, ch, 1, part(st, ch, 0, 0), part(st, ch, 0, 1), left)
         spread("c0", st, ch, 2, part(st, ch, 0, 0), part(st, ch, 1, 0), partner)
@@ -233,13 +254,13 @@
     def stage_d(st, ch):
         for name in ("c0", "c1", "c3", "c2"):
             copies[name, st, ch].wait_recv()
-        arrived = rows[st, ch]
+        arrived = rows[st, :, cols(st, ch)]
         if st == 0:
             if ch == 0:
                 need("wg")
                 need("wu")
-            gate = jnp.dot(arrived, wg[cols(ch), :], preferred_element_type=jnp.float32)
-            up = jnp.dot(arrived, wu[cols(ch), :], preferred_element_type=jnp.float32)
+            gate = jnp.dot(arrived, wg[cols(st, ch), :], preferred_element_type=jnp.float32)
+            up = jnp.dot(arrived, wu[cols(st, ch), :], preferred_element_type=jnp.float32)
             if ch == 0:
                 gacc[...] = gate
                 uacc[...] = up
@@ -249,7 +270,7 @@
         else:
             if ch == 0:
                 need("wd")
-            grad = lax.dot_general(arrived, wd[:, cols(ch)], LAST, preferred_element_type=jnp.float32)
+            grad = lax.dot_general(arrived, wd[:, cols(st, ch)], LAST, preferred_element_type=jnp.float32)
             if ch == 0:
                 hacc[...] = grad
             else:
@@ -290,63 +311,61 @@
         if st == 0:
             if ch == 0:
                 need("wd")
-            partial = jnp.dot(hid[...], wd[:, cols(ch)], preferred_element_type=jnp.float32)
+            partial = jnp.dot(hid[...], wd[:, cols(st, ch)], preferred_element_type=jnp.float32)
         else:
             partial = lax.dot_general(
-                ggrad[...], wg[cols(ch), :], LAST, preferred_element_type=jnp.float32
+                ggrad[...], wg[cols(st, ch), :], LAST, preferred_element_type=jnp.float32
             )
             partial = partial + lax.dot_general(
-                ugrad[...], wu[cols(ch), :], LAST, preferred_element_type=jnp.float32
+                ugrad[...], wu[cols(st, ch), :], LAST, preferred_element_type=jnp.float32
             )
-        psend[st, ch] = partial[side:, :].astype(jnp.bfloat16)
-        back("p", st, ch, 0, psend.at[st, ch], precv.at[st, ch], partner)
-        pown[st, ch] = partial[:side, :]
+        psend[st, :, cols(st, ch)] = partial[side:, :].astype(jnp.bfloat16)
+        here = cols(st, ch)
+        back("p", st, ch, 0, psend.at[st, :, here], precv.at[st, :, here], partner)
+        pown[st, :, cols(st, ch)] = partial[:side, :]
+
+    def chip_sum(st, delta, some):
+        lines = pl.ds(delta * block, block)
+        return pown[st, lines, some] + precv[st, lines, some].astype(jnp.float32)
 
     def stage_f(st, ch):
         copies["p", st, ch].wait_recv()
-        far_rows = pl.ds(2 * block, block)
-        t2s[st, ch] = (
-            pown[st, ch, far_rows, :] + precv[st, ch, far_rows, :].astype(jnp.float32)
-        ).astype(jnp.bfloat16)
-        a, b = pl.ds(0, half), pl.ds(half, half)
-        back("tl", st, ch, 1, t2s.at[st, ch, :, a], t2r.at[st, ch, :, a], left)
-        back("tr", st, ch, 2, t2s.at[st, ch, :, b], t2r.at[st, ch, :, b], right)
-
-    def chip_sum(st, ch, delta):
-        some = pl.ds(delta * block, block)
-        return pown[st, ch, some, :] + precv[st, ch, some, :].astype(jnp.float32)
+        t2s[st, :, cols(st, ch)] = chip_sum(st, 2, cols(st, ch)).astype(jnp.bfloat16)
+        a, b = low(st, ch), high(st, ch)
+        back("tl", st, ch, 1, t2s.at[st, :, a], t2r.at[st, :, a], left)
+        back("tr", st, ch, 2, t2s.at[st, :, b], t2r.at[st, :, b], right)
 
     def stage_g(st, ch):
-        to_left = chip_sum(st, ch, 3)
+        here, a, b = cols(st, ch), low(st, ch), high(st, ch)
+        ts[st, 0, :, b] = chip_sum(st, 3, b).astype(jnp.bfloat16)
         copies["tl", st, ch].wait_recv()
-        ts[st, ch, 0, :, 0:half] = (
-            to_left[:, :half] + t2r[st, ch, :, 0:half].astype(jnp.float32)
-        ).astype(jnp.bfloat16)
-        ts[st, ch, 0, :, half:wide] = to_left[:, half:].astype(jnp.bfloat16)
-        back("sl", st, ch, 3, ts.at[st, ch, 0], tr.at[st, ch, 0], left)
-        to_right = chip_sum(st, ch, 1)
+        ts[st, 0, :, a] = (chip_sum(st, 3, a) + t2r[st, :, a].astype(jnp.float32)).astype(
+            jnp.bfloat16
+        )
+        back("sl", st, ch, 3, ts.at[st, 0, :, here], tr.at[st, 0, :, here], left)
+        ts[st, 1, :, a] = chip_sum(st, 1, a).astype(jnp.bfloat16)
         copies["tr", st, ch].wait_recv()
-        ts[st, ch, 1, :, 0:half] = to_right[:, :half].astype(jnp.bfloat16)
-        ts[st, ch, 1, :, half:wide] = (
-            to_right[:, half:] + t2r[st, ch, :, half:wide].astype(jnp.float32)
-        ).astype(jnp.bfloat16)
-        back("sr", st, ch, 4, ts.at[st, ch, 1], tr.at[st, ch, 1], right)
+        ts[st, 1, :, b] = (chip_sum(st, 1, b) + t2r[st, :, b].astype(jnp.float32)).astype(
+            jnp.bfloat16
+        )
+        back("sr", st, ch, 4, ts.at[st, 1, :, here], tr.at[st, 1, :, here], right)
 
     def stage_h(st, ch):
-        own = chip_sum(st, ch, 0)
+        here = cols(st, ch)
         copies["sl", st, ch].wait_recv()
         copies["sr", st, ch].wait_recv()
-        own = own + tr[st, ch, 0].astype(jnp.float32) + tr[st, ch, 1].astype(jnp.float32)
+        own = chip_sum(st, 0, here) + tr[st, 0, :, here].astype(jnp.float32)
+        own = own + tr[st, 1, :, here].astype(jnp.float32)
         for d in range(EXPERTS):
             piece = own[d * CAP : (d + 1) * CAP, :].astype(jnp.bfloat16)
             if d == 0:
-                hr[st, ch, 0] = piece
+                hr[st, 0, :, here] = piece
             else:
-                hs[st, ch, d] = piece
+                hs[st, d, :, here] = piece
         for d in range(1, EXPERTS):
             copy = remote(
-                hs.at[st, ch, d],
-                hr.at[st, ch, d],
+                hs.at[st, d, :, here],
+                hr.at[st, d, :, here],
                 h_ss.at[st, ch, d],
                 h_rs.at[st, ch, d],
                 source_of(d),
@@ -357,8 +376,8 @@
     def handoff(st, ch):
         to = section + 1 if st == 0 else section - 1
         return remote(
-            osend.at[st, ch],
-            outs[st].at[0, :, cols(ch)],
+            osend.at[st, :, cols(st, ch)],
+            outs[st].at[0, :, cols(st, ch)],
             z_ss.at[st, ch],
             z_rs.at[st, ch],
             (to, place),
@@ -373,60 +392,52 @@
     def stage_i(st, ch):
         for d in range(1, EXPERTS):
             copies["h", st, ch, d].wait_recv()
-        base = tok[st, :, cols(ch)].astype(jnp.float32)
+        base = tok[st, :, cols(st, ch)].astype(jnp.float32)
         lines = []
         for t in range(TOK):
             total = None
             for d in range(EXPERTS):
-                term = join_table[st][t][d][:, 0:1] * hr[st, ch, d].astype(jnp.float32)
+                term = join_table[st][t][d][:, 0:1] * hr[st, d, :, cols(st, ch)].astype(jnp.float32)
                 total = term if total is None else total + term
             lines.append(base[t : t + 1, :] + total[0:1, :] + total[1:2, :])
-        osend[st, ch] = jnp.concatenate(lines, axis=0).astype(jnp.bfloat16)
+        osend[st, :, cols(st, ch)] = jnp.concatenate(lines, axis=0).astype(jnp.bfloat16)
 
         @pl.when(gives(st))
         def _():
             handoff(st, ch).start()
 
-    chunks = [(st, ch) for st in range(2) for ch in range(cuts)]
-    need("act")
-    for ch in range(cuts):
-        pack(0, ch)
     ends = (section + 1 < sections).astype(jnp.int32) + (section > 0).astype(jnp.int32)
-    pl.semaphore_wait(barrier, EXPERTS - 1 + 3 + ends)
-
-    for ch in range(cuts):
-        send_slots(0, ch)
-    need("cot")
-    for ch in range(cuts):
-        pack(1, ch)
-        send_slots(1, ch)
-
-    stages = (
-        (stage_a, 0),
-        (stage_b, 1),
-        (stage_c, 2),
-        (stage_d, 3),
-        (stage_e, cuts + 3),
-        (stage_f, cuts + 4),
-        (stage_g, cuts + 5),
-        (stage_h, cuts + 6),
-        (stage_i, cuts + 8),
-    )
-    total_steps = len(chunks) + stages[-1][1]
-    for step in range(total_steps):
-        for stage, lag in stages:
-            number = step - lag
-            if 0 <= number < len(chunks):
-                st, ch = chunks[number]
-                stage(st, ch)
-                if stage is stage_d and ch == cuts - 1:
-                    middle(st)
+    stages = {
+        "A": stage_a,
+        "B": stage_b,
+        "C": stage_c,
+        "D": stage_d,
+        "E": stage_e,
+        "F": stage_f,
+        "G": stage_g,
+        "H": stage_h,
+        "I": stage_i,
+    }
+    greeted = False
+    for step in order:
+        kind, st, ch = step[0], int(step[1]), int(step[2])
+        if kind == "P":
+            need("act" if st == 0 else "cot")
+            pack(st, ch)
+            if not greeted:
+                pl.semaphore_wait(barrier, EXPERTS - 1 + 3 + ends)
+                greeted = True
+            send_slots(st, ch)
+        elif kind == "M":
+            middle(st)
+        else:
+            stages[kind](st, ch)
 
     for st in range(2):
 
         @pl.when(takes(st))
         def _():
-            for ch in range(cuts):
+            for ch in range(len(widths[st])):
                 handoff(st, ch).wait_recv()
 
         @pl.when(jnp.logical_not(takes(st)))
@@ -435,7 +446,7 @@
 
         @pl.when(gives(st))
         def _():
-            for ch in range(cuts):
+            for ch in range(len(widths[st])):
                 handoff(st, ch).wait_send()
 
     for copy in copies.values():
@@ -455,11 +466,10 @@
     saved_gate,
     saved_up,
 ):
-    cuts = CHUNKS
+    cuts = max(len(WIDTHS[0]), len(WIDTHS[1]))
     tokens, width = activations.shape[1:]
     units = gate_weight.shape[1]
     slots = saved_gate.shape[1]
-    wide = width // cuts
     block = EXPERTS * CAP
     side = RING * block
     anywhere = pl.BlockSpec(memory_space=pl.ANY)
@@ -470,7 +480,7 @@
     dma = pltpu.SemaphoreType.DMA
     out = jax.ShapeDtypeStruct(activations.shape, half)
     return pl.pallas_call(
-        functools.partial(kernel, cuts),
+        functools.partial(kernel, WIDTHS, ORDER),
         out_shape=(out, out),
         in_specs=[anywhere, anywhere, scalar, scalar, scalar, scalar] + [anywhere] * 5,
         out_specs=(vmem, vmem),
@@ -481,25 +491,25 @@
             pltpu.VMEM((units, width), half),
             pltpu.VMEM((slots, units), half),
             pltpu.VMEM((slots, units), half),
-            pltpu.VMEM((2, cuts, EXPERTS, CAP, wide), half),
-            pltpu.VMEM((2, cuts, EXPERTS, CAP, wide), half),
-            pltpu.VMEM((2, cuts, slots, wide), half),
+            pltpu.VMEM((2, EXPERTS, CAP, width), half),
+            pltpu.VMEM((2, EXPERTS, CAP, width), half),
+            pltpu.VMEM((2, slots, width), half),
             pltpu.VMEM((slots, units), full),
             pltpu.VMEM((slots, units), full),
             pltpu.VMEM((slots, units), full),
             pltpu.VMEM((slots, units), half),
             pltpu.VMEM((slots, units), half),
             pltpu.VMEM((slots, units), half),
-            pltpu.VMEM((2, cuts, side, wide), half),
-            pltpu.VMEM((2, cuts, side, wide), half),
-            pltpu.VMEM((2, cuts, side, wide), full),
-            pltpu.VMEM((2, cuts, block, wide), half),
-            pltpu.VMEM((2, cuts, block, wide), half),
-            pltpu.VMEM((2, cuts, 2, block, wide), half),
-            pltpu.VMEM((2, cuts, 2, block, wide), half),
-            pltpu.VMEM((2, cuts, EXPERTS, CAP, wide), half),
-            pltpu.VMEM((2, cuts, EXPERTS, CAP, wide), half),
-            pltpu.VMEM((2, cuts, tokens, wide), half),
+            pltpu.VMEM((2, side, width), half),
+            pltpu.VMEM((2, side, width), half),
+            pltpu.VMEM((2, side, width), full),
+            pltpu.VMEM((2, block, width), half),
+            pltpu.VMEM((2, block, width), half),
+            pltpu.VMEM((2, 2, block, width), half),
+            pltpu.VMEM((2, 2, block, width), half),
+            pltpu.VMEM((2, EXPERTS, CAP, width), half),
+            pltpu.VMEM((2, EXPERTS, CAP, width), half),
+            pltpu.VMEM((2, tokens, width), half),
             dma((7,)),
             dma((2, cuts, EXPERTS)),
             dma((2, cuts, EXPERTS)),
@@ -518,10 +528,10 @@
     )(
         activations,
         cotangent,
-        forward_experts,
-        forward_weights,
-        backward_experts,
-        backward_weights,
+        forward_experts.transpose(1, 0, 2),
+        forward_weights.transpose(1, 0, 2),
+        backward_experts.transpose(1, 0, 2),
+        backward_weights.transpose(1, 0, 2),
         gate_weight,
         up_weight,
         down_weight,

time: 87.3 us -> 69.8 us (0.80)
  Pallas kernels: 78.3 us -> 66 us
  local copies, waits for them, and re-layouts: 7.96 us -> 2.92 us
    pallas_call x1, Pallas kernels: 78.3 us -> 66 us  [body(): pl.pallas_call(functools.partial(kernel, WIDTHS, ORDER), out_shape=(out,...]
    unnamed x6 -> x2, local copies, waits for them, and re-layouts: 7.96 us -> 2.92 us
where the time goes in v2:
time: 69.8 us; the launch traced here: 69.6 us
  Pallas kernels  66 us (95%)
  local copies, waits for them, and re-layouts  2.92 us (4%)
    pallas_call x1, Pallas kernels, body(): pl.pallas_call(functools.partial(kernel, WIDTHS, ORDER), out_shape=(out,...  66 us
    unnamed x2, local copies, waits for them, and re-layouts  2.92 us

profile of v2, /device:TPU:192, one launch (start us, length us, event | category | flops | bytes accessed | tf_op | source)
XLA Modules:
  0.0 69.6 jit_solution(3215455645759073804)
XLA Ops:
  0.6 66.0 %shard_map.122 = (bf16[1,3,7168]{2,1,0:T(4,128)(2,1)}, bf16[1,3,7168]{2,1,0:T(4,128)(2,1)}) custom-call(bf16[1,3,7168]{2,1,0:T(4,128)(2,1)} %act_hbm.1, bf16[1,3,7168]{2,1,0:T(4,128)(2,1)} %cot_hbm.1, s32[3,1,4]{2,1,0:T(1,128)} %bitcast.4, f32[3,1,4]{2,1,0:T(1,128)} %bitcast.5, s32[3,1,4]{2,1,0:T(1,128)} %bitcast.6, f32[3,1,4]{2,1,0:T(1,128)} %bitcast.7, ...), custom_call_target="tpu_custom_call" | custom-call | tf_op jit(solution)/shard_map/pallas_call | solution.py:482
  66.7 1.5 %copy.15 = bf16[1,3,7168]{2,1,0:T(4,128)(2,1)} copy(bf16[1,3,7168]{2,1,0:T(4,128)(2,1)} %get-tuple-element.4) | data formatting | bytes 86016
  68.1 1.5 %copy.16 = bf16[1,3,7168]{2,1,0:T(4,128)(2,1)} copy(bf16[1,3,7168]{2,1,0:T(4,128)(2,1)} %get-tuple-element.5) | data formatting | bytes 86016

commit v3 on v2

--- a/solution.py
+++ b/solution.py
@@ -13,15 +13,16 @@
 TOK = 3
 CORES = 2
 RING = 4
-WIDTHS = ((1792, 1792, 1792, 1792), (1792, 1792, 1792, 1792))
+WIDTHS = ((2304, 2560, 2304), (2304, 2560, 2304))
+FAR = ((0,) * 8, (0,) * 8)
+FARB = ((0,) * 8, (0,) * 8)
 ORDER = (
-    "P00", "P01", "P02", "P03", "P10", "P11", "P12", "P13", "A00", "A01", "A02", "B00",
-    "A03", "B01", "A10", "B02", "C00", "A11", "B03", "D00", "C01", "A12", "B10", "D01",
-    "C02", "A13", "B11", "D02", "C03", "B12", "D03", "M00", "C10", "E00", "E01", "B13",
-    "E02", "C11", "E03", "C12", "F00", "D10", "F01", "C13", "F02", "D11", "G00", "F03",
-    "G01", "D12", "D13", "M10", "G02", "E10", "E11", "H00", "E12", "G03", "E13", "F10",
-    "H01", "F11", "H02", "F12", "F13", "H03", "G10", "G11", "I00", "G12", "G13", "I01",
-    "H10", "I02", "H11", "H12", "I03", "H13", "I10", "I11", "I12", "I13",
+    "P00", "P01", "P02", "P10", "A00", "P11", "A01", "P12", "A02", "B00", "A10", "B01",
+    "B02", "C00", "A11", "A12", "C01", "C02", "D00", "B10", "D01", "D02", "B11", "M00",
+    "E00", "B12", "C10", "E01", "F00", "C11", "D10", "C12", "E02", "F01", "D11", "G00",
+    "D12", "M10", "F02", "E10", "G01", "E11", "E12", "F10", "G02", "F11", "H00", "F12",
+    "G10", "H01", "H02", "G11", "G12", "H10", "H11", "H12", "I02", "I00", "I10", "I01",
+    "I11", "I12",
 )
 MESH = pl.DeviceIdType.MESH
 LAST = (((1,), (1,)), ((), ()))
@@ -67,7 +68,9 @@
     tr,
     hs,
     hr,
-    osend,
+    base,
+    tsend,
+    trecv,
     in_sem,
     y_ss,
     y_rs,
@@ -77,8 +80,8 @@
     r_rs,
     h_ss,
     h_rs,
-    z_ss,
-    z_rs,
+    b_ss,
+    b_rs,
 ):
     sections = lax.axis_size("pipe")
     section = lax.axis_index("pipe")
@@ -96,12 +99,28 @@
     right = at(y, (x + 1) % RING, c)
     left = at(y, (x + RING - 1) % RING, c)
     partner = at(y, x, 1 - c)
+    opposite = at(y, (x + 2) % RING, c)
 
     def expert_of(d):
         return at((y + EXPERTS - d) % EXPERTS, x, c)
 
-    def source_of(d):
-        return at((y + d) % EXPERTS, x, c)
+    def ahead(st):
+        return section + 1 if st == 0 else section - 1
+
+    def behind(st):
+        return section - 1 if st == 0 else section + 1
+
+    def gives(st):
+        return section + 1 < sections if st == 0 else section > 0
+
+    def takes(st):
+        return section > 0 if st == 0 else section + 1 < sections
+
+    def heir_of(st, d):
+        return (ahead(st), (((y + d) % EXPERTS) * RING + x) * CORES + c)
+
+    def giver_of(st, d):
+        return (behind(st), (((y + EXPERTS - d) % EXPERTS) * RING + x) * CORES + c)
 
     def wide(st, ch):
         return widths[st][ch]
@@ -157,13 +176,20 @@
     greet(left)
     greet(partner)
 
-    @pl.when(section + 1 < sections)
-    def _():
-        greet((section + 1, place))
-
-    @pl.when(section > 0)
-    def _():
-        greet((section - 1, place))
+    greet(opposite)
+    for st in range(2):
+
+        @pl.when(gives(st))
+        def _():
+            for d in range(EXPERTS):
+                greet(heir_of(st, d))
+
+    for st in range(2):
+
+        @pl.when(takes(st))
+        def _():
+            for d in range(EXPERTS):
+                greet(giver_of(st, d))
 
     shape = (EXPERTS, CAP, 128)
     far = lax.broadcasted_iota(jnp.int32, shape, 0)
@@ -189,7 +215,9 @@
     plain_f, weighted_f = tables(fexp, fwt)
     plain_b, weighted_b = tables(bexp, bwt)
     pack_table = (plain_f, weighted_b)
-    join_table = (weighted_f, plain_b)
+    for t in range(TOK):
+        tsend[0, t] = weighted_f[t]
+        tsend[1, t] = plain_b[t]
 
     copies = {}
 
@@ -236,19 +264,23 @@
         rows[st, 0:block, cols(st, ch)] = own.astype(jnp.bfloat16)
         spread("xr", st, ch, 0, part(st, ch, 0, 0), part(st, ch, 0, 3), right)
         spread("xl", st, ch, 1, part(st, ch, 0, 0), part(st, ch, 0, 1), left)
+        if FAR[st][ch]:
+            spread("xo", st, ch, 3, part(st, ch, 0, 0), part(st, ch, 0, 2), opposite)
         spread("c0", st, ch, 2, part(st, ch, 0, 0), part(st, ch, 1, 0), partner)
 
     def stage_b(st, ch):
         copies["xl", st, ch].wait_recv()
-        spread("hl", st, ch, 3, halfpart(st, ch, 0, 1, 0), halfpart(st, ch, 0, 2, 0), left)
+        if not FAR[st][ch]:
+            spread("hl", st, ch, 3, halfpart(st, ch, 0, 1, 0), halfpart(st, ch, 0, 2, 0), left)
         copies["xr", st, ch].wait_recv()
-        spread("hr", st, ch, 4, halfpart(st, ch, 0, 3, 1), halfpart(st, ch, 0, 2, 1), right)
+        if not FAR[st][ch]:
+            spread("hr", st, ch, 4, halfpart(st, ch, 0, 3, 1), halfpart(st, ch, 0, 2, 1), right)
         spread("c1", st, ch, 5, part(st, ch, 0, 1), part(st, ch, 1, 1), partner)
         spread("c3", st, ch, 6, part(st, ch, 0, 3), part(st, ch, 1, 3), partner)
 
     def stage_c(st, ch):
-        copies["hl", st, ch].wait_recv()
-        copies["hr", st, ch].wait_recv()
+        for name in ("xo",) if FAR[st][ch] else ("hl", "hr"):
+            copies[name, st, ch].wait_recv()
         spread("c2", st, ch, 7, part(st, ch, 0, 2), part(st, ch, 1, 2), partner)
 
     def stage_d(st, ch):
@@ -330,12 +362,22 @@
 
     def stage_f(st, ch):
         copies["p", st, ch].wait_recv()
-        t2s[st, :, cols(st, ch)] = chip_sum(st, 2, cols(st, ch)).astype(jnp.bfloat16)
-        a, b = low(st, ch), high(st, ch)
-        back("tl", st, ch, 1, t2s.at[st, :, a], t2r.at[st, :, a], left)
-        back("tr", st, ch, 2, t2s.at[st, :, b], t2r.at[st, :, b], right)
+        here = cols(st, ch)
+        t2s[st, :, here] = chip_sum(st, 2, here).astype(jnp.bfloat16)
+        if FARB[st][ch]:
+            back("to", st, ch, 1, t2s.at[st, :, here], t2r.at[st, :, here], opposite)
+            ts[st, 0, :, here] = chip_sum(st, 3, here).astype(jnp.bfloat16)
+            back("sl", st, ch, 3, ts.at[st, 0, :, here], tr.at[st, 0, :, here], left)
+            ts[st, 1, :, here] = chip_sum(st, 1, here).astype(jnp.bfloat16)
+            back("sr", st, ch, 4, ts.at[st, 1, :, here], tr.at[st, 1, :, here], right)
+        else:
+            a, b = low(st, ch), high(st, ch)
+            back("tl", st, ch, 1, t2s.at[st, :, a], t2r.at[st, :, a], left)
+            back("tr", st, ch, 2, t2s.at[st, :, b], t2r.at[st, :, b], right)
 
     def stage_g(st, ch):
+        if FARB[st][ch]:
+            return
         here, a, b = cols(st, ch), low(st, ch), high(st, ch)
         ts[st, 0, :, b] = chip_sum(st, 3, b).astype(jnp.bfloat16)
         copies["tl", st, ch].wait_recv()
@@ -356,55 +398,56 @@
         copies["sr", st, ch].wait_recv()
         own = chip_sum(st, 0, here) + tr[st, 0, :, here].astype(jnp.float32)
         own = own + tr[st, 1, :, here].astype(jnp.float32)
+        if FARB[st][ch]:
+            copies["to", st, ch].wait_recv()
+            own = own + t2r[st, :, here].astype(jnp.float32)
         for d in range(EXPERTS):
-            piece = own[d * CAP : (d + 1) * CAP, :].astype(jnp.bfloat16)
-            if d == 0:
-                hr[st, 0, :, here] = piece
-            else:
-                hs[st, d, :, here] = piece
-        for d in range(1, EXPERTS):
-            copy = remote(
-                hs.at[st, d, :, here],
-                hr.at[st, d, :, here],
-                h_ss.at[st, ch, d],
-                h_rs.at[st, ch, d],
-                source_of(d),
-            )
-            copy.start()
-            copies["h", st, ch, d] = copy
-
-    def handoff(st, ch):
-        to = section + 1 if st == 0 else section - 1
-        return remote(
-            osend.at[st, :, cols(st, ch)],
-            outs[st].at[0, :, cols(st, ch)],
-            z_ss.at[st, ch],
-            z_rs.at[st, ch],
-            (to, place),
-        )
-
-    def gives(st):
-        return section + 1 < sections if st == 0 else section > 0
-
-    def takes(st):
-        return section > 0 if st == 0 else section + 1 < sections
-
-    def stage_i(st, ch):
-        for d in range(1, EXPERTS):
-            copies["h", st, ch, d].wait_recv()
-        base = tok[st, :, cols(st, ch)].astype(jnp.float32)
-        lines = []
-        for t in range(TOK):
-            total = None
-            for d in range(EXPERTS):
-                term = join_table[st][t][d][:, 0:1] * hr[st, d, :, cols(st, ch)].astype(jnp.float32)
-                total = term if total is None else total + term
-            lines.append(base[t : t + 1, :] + total[0:1, :] + total[1:2, :])
-        osend[st, :, cols(st, ch)] = jnp.concatenate(lines, axis=0).astype(jnp.bfloat16)
+            hs[st, d, :, here] = own[d * CAP : (d + 1) * CAP, :].astype(jnp.bfloat16)
 
         @pl.when(gives(st))
         def _():
-            handoff(st, ch).start()
+            for d in range(EXPERTS):
+                homeward(st, ch, d).start()
+
+    def homeward(st, ch, d):
+        here = cols(st, ch)
+        return remote(
+            hs.at[st, d, :, here],
+            hr.at[st, d, :, here],
+            h_ss.at[st, ch, d],
+            h_rs.at[st, ch, d],
+            heir_of(st, d),
+        )
+
+    def footing(st):
+        to = (ahead(st), place)
+        return (
+            remote(tok.at[st], base.at[st], b_ss.at[st, 0], b_rs.at[st, 0], to),
+            remote(tsend.at[st], trecv.at[st], b_ss.at[st, 1], b_rs.at[st, 1], to),
+        )
+
+    def stage_i(st, ch):
+        here = cols(st, ch)
+
+        @pl.when(takes(st))
+        def _():
+            if ("base", st) not in seen_base:
+                seen_base.add(("base", st))
+                for copy in footing(st):
+                    copy.wait_recv()
+            for d in range(EXPERTS):
+                homeward(st, ch, d).wait_recv()
+            ground = base[st, :, here].astype(jnp.float32)
+            lines = []
+            for t in range(TOK):
+                total = None
+                for d in range(EXPERTS):
+                    term = trecv[st, t, d][:, 0:1] * hr[st, d, :, here].astype(jnp.float32)
+                    total = term if total is None else total + term
+                lines.append(ground[t : t + 1, :] + total[0:1, :] + total[1:2, :])
+            outs[st][0, :, here] = jnp.concatenate(lines, axis=0).astype(jnp.bfloat16)
+
+    seen_base = set()
 
     ends = (section + 1 < sections).astype(jnp.int32) + (section > 0).astype(jnp.int32)
     stages = {
@@ -425,9 +468,16 @@
             need("act" if st == 0 else "cot")
             pack(st, ch)
             if not greeted:
-                pl.semaphore_wait(barrier, EXPERTS - 1 + 3 + ends)
+                pl.semaphore_wait(barrier, EXPERTS - 1 + 4 + 2 * EXPERTS * ends)
                 greeted = True
             send_slots(st, ch)
+            if ch == len(widths[st]) - 1:
+
+                @pl.when(gives(st))
+                def _():
+                    for copy in footing(st):
+                        copy.start()
+
         elif kind == "M":
             middle(st)
         else:
@@ -435,22 +485,25 @@
 
     for st in range(2):
 
-        @pl.when(takes(st))
-        def _():
-            for ch in range(len(widths[st])):
-                handoff(st, ch).wait_recv()
-
         @pl.when(jnp.logical_not(takes(st)))
         def _():
             outs[st][...] = jnp.zeros_like(outs[st])
 
         @pl.when(gives(st))
         def _():
+            for copy in footing(st):
+                copy.wait_send()
             for ch in range(len(widths[st])):
-                handoff(st, ch).wait_send()
+                for d in range(EXPERTS):
+                    homeward(st, ch, d).wait_send()
 
     for copy in copies.values():
         copy.wait_send()
+
+
+def settle(first, second, first_out, second_out):
+    first_out[...] = first[...]
+    second_out[...] = second[...]
 
 
 def body(
@@ -479,7 +532,7 @@
     full = jnp.float32
     dma = pltpu.SemaphoreType.DMA
     out = jax.ShapeDtypeStruct(activations.shape, half)
-    return pl.pallas_call(
+    results = pl.pallas_call(
         functools.partial(kernel, WIDTHS, ORDER),
         out_shape=(out, out),
         in_specs=[anywhere, anywhere, scalar, scalar, scalar, scalar] + [anywhere] * 5,
@@ -510,6 +563,8 @@
             pltpu.VMEM((2, EXPERTS, CAP, width), half),
             pltpu.VMEM((2, EXPERTS, CAP, width), half),
             pltpu.VMEM((2, tokens, width), half),
+            pltpu.VMEM((2, tokens, EXPERTS, CAP, 128), full),
+            pltpu.VMEM((2, tokens, EXPERTS, CAP, 128), full),
             dma((7,)),
             dma((2, cuts, EXPERTS)),
             dma((2, cuts, EXPERTS)),
@@ -519,8 +574,8 @@
             dma((2, cuts, 5)),
             dma((2, cuts, EXPERTS)),
             dma((2, cuts, EXPERTS)),
-            dma((2, cuts)),
-            dma((2, cuts)),
+            dma((2, 2)),
+            dma((2, 2)),
         ],
         compiler_params=pltpu.CompilerParams(
             collective_id=0, has_side_effects=True, vmem_limit_bytes=60 * 1024 * 1024
@@ -538,6 +593,12 @@
         saved_gate,
         saved_up,
     )
+    return pl.pallas_call(
+        settle,
+        out_shape=(out, out),
+        in_specs=[vmem, vmem],
+        out_specs=(vmem, vmem),
+    )(*results)
 
 
 def solution(mesh):

time: 69.8 us -> 66.9 us (0.958)
  local copies, waits for them, and re-layouts: 2.92 us -> 0 us
    unnamed x2 -> x0, local copies, waits for them, and re-layouts: 2.92 us -> none
    pallas_call x0 -> x1, Pallas kernels: none -> 1.5 us  [body(): pl.pallas_call(settle, out_shape=(out, out), in_specs=[vmem, vmem], out_s...]
    pallas_call x1, Pallas kernels: 66 us -> 64.5 us  [body(): pl.pallas_call(functools.partial(kernel, WIDTHS, ORDER), out_shape=(out,...]
where the time goes in v3:
time: 66.9 us; the launch traced here: 66.7 us
  Pallas kernels  66 us (99%)
    pallas_call x1, Pallas kernels, body(): pl.pallas_call(functools.partial(kernel, WIDTHS, ORDER), out_shape=(out,...  64.5 us
    pallas_call x1, Pallas kernels, body(): pl.pallas_call(settle, out_shape=(out, out), in_specs=[vmem, vmem], out_s...  1.5 us

profile of v3, /device:TPU:192, one launch (start us, length us, event | category | flops | bytes accessed | tf_op | source)
XLA Modules:
  0.0 66.7 jit_solution(5145741052846025861)
XLA Ops:
  0.6 64.5 %shard_map.122 = (bf16[1,3,7168]{2,1,0:T(4,128)(2,1)}, bf16[1,3,7168]{2,1,0:T(4,128)(2,1)}) custom-call(bf16[1,3,7168]{2,1,0:T(4,128)(2,1)} %act_hbm.1, bf16[1,3,7168]{2,1,0:T(4,128)(2,1)} %cot_hbm.1, s32[3,1,4]{2,1,0:T(1,128)} %bitcast.4, f32[3,1,4]{2,1,0:T(1,128)} %bitcast.5, s32[3,1,4]{2,1,0:T(1,128)} %bitcast.6, f32[3,1,4]{2,1,0:T(1,128)} %bitcast.7, ...), custom_call_target="tpu_custom_call" | custom-call | tf_op jit(solution)/shard_map/pallas_call | solution.py:535
  65.2 1.5 %shard_map.123 = (bf16[1,3,7168]{2,1,0:T(4,128)(2,1)}, bf16[1,3,7168]{2,1,0:T(4,128)(2,1)}) custom-call(bf16[1,3,7168]{2,1,0:T(4,128)(2,1)} %get-tuple-element.4.first, bf16[1,3,7168]{2,1,0:T(4,128)(2,1)} %get-tuple-element.5.second), custom_call_target="tpu_custom_call" | custom-call | tf_op jit(solution)/shard_map/pallas_call | solution.py:596
